TPU v7x, 512 devices: a whole 4x4x16 slice. The times are simulated.
512 devices in a mesh: cp: 64 (over y, x, z_lo), sp: 8 (over z_hi, core).
Axes of the slice: x: 4, y: 4, z: 16 (z_hi: 4, z_lo: 4; z = z_hi * 4 + z_lo), core: 2. Of those that a mesh axis runs over, the one named last changes fastest.
Arguments:
- queries: bfloat16 [16384, 2048], P('cp', 'sp'), may hold values from -22 to 22
- keys: bfloat16 [16384, 128], P(('cp', 'sp')), may hold values from -5 to 5
- values: bfloat16 [16384, 128], P(('cp', 'sp')), may hold values from -6 to 6
- doc_ids: int32 [128], replicated, may hold values from 0 to 31, never falling along the last dimension, each value on 1 to 32 neighbouring positions
- span_order: int32 [64], replicated, may hold values from 0 to 63, each once
Outputs:
- attended: bfloat16 [16384, 2048], P('cp', 'sp')
Inputs may be any that keep to these rules, and one draw needn't show every extreme that they name: doc_ids never falls; each document covers 1 to 32 consecutive blocks, and one covers exactly 32. Index i of cp holds span span_order[i] of the sequence; each span once.
All inputs are finite; a program needn't handle non-finite values.
Results may differ from a plain program's by a relative error of at most 0.0036.
Values may be sent and summed in bfloat16 or wider, within the bound.
A program may use at most 64 MiB of HBM per device.

v0:
```python
import math
import jax
import jax.numpy as jnp
from jax import lax
from jax.sharding import PartitionSpec as P

HD = 128
SPAN = 256
BLK = 128
NEGATIVE = -1e30


def true_position(row_ids, span_order):
    span_index = row_ids // SPAN
    lookup = jnp.arange(span_order.shape[0], dtype=jnp.int32)
    placed = jnp.sum(
        jnp.where(span_index[:, None] == lookup[None, :], span_order[None, :], 0), axis=1
    )
    return placed * SPAN + row_ids % SPAN


def doc_lookup(position, doc_ids):
    block_index = position // BLK
    lookup = jnp.arange(doc_ids.shape[0], dtype=jnp.int32)
    return jnp.sum(jnp.where(block_index[:, None] == lookup[None, :], doc_ids[None, :], 0), axis=1)


def make_folder(query_block, query_pos, query_doc, span_order, doc_ids):
    score_scale = 1.0 / math.sqrt(query_block.shape[2])

    def fold_piece(carried, piece, start):
        key_piece, value_piece = piece
        piece_rows = key_piece.shape[0]
        tile_rows = math.gcd(piece_rows, SPAN)
        tile_count = piece_rows // tile_rows
        key_tiles = key_piece.reshape(tile_count, tile_rows, key_piece.shape[1])
        value_tiles = value_piece.reshape(tile_count, tile_rows, value_piece.shape[1])

        def tile_step(state_now, tile_inputs):
            key_tile, value_tile, tile_index = tile_inputs
            row_ids = tile_index * tile_rows + jnp.arange(tile_rows, dtype=jnp.int32)
            key_pos = true_position(row_ids, span_order)
            key_doc = doc_lookup(key_pos, doc_ids)
            allowed = (key_pos[None, :] <= query_pos[:, None]) & (
                key_doc[None, :] == query_doc[:, None]
            )
            run_max, run_total, run_accum = state_now
            scores = (
                jnp.einsum("rhd,kd->hrk", query_block, key_tile, preferred_element_type=jnp.float32)
                * score_scale
            )
            masked = jnp.where(allowed[None], scores, NEGATIVE)
            new_max = jnp.maximum(run_max, jnp.max(masked, axis=2))
            rescale = jnp.exp(run_max - new_max)
            weights = jnp.where(allowed[None], jnp.exp(masked - new_max[:, :, None]), 0.0)
            new_total = run_total * rescale + jnp.sum(weights, axis=2)
            product = jnp.einsum(
                "hrk,kd->rhd",
                weights.astype(jnp.bfloat16),
                value_tile,
                preferred_element_type=jnp.float32,
            )
            new_accum = run_accum * jnp.transpose(rescale)[:, :, None] + product
            result = (new_max, new_total, new_accum)
            return (result, None)

        tile_ids = jnp.arange(tile_count, dtype=jnp.int32)
        carried, unused = lax.scan(tile_step, carried, (key_tiles, value_tiles, tile_ids))
        return carried

    return fold_piece


def shards(queries, keys, values, doc_ids, span_order):
    cp_index = lax.axis_index("cp")
    query_ids = cp_index * SPAN + jnp.arange(queries.shape[0], dtype=jnp.int32)
    query_count = queries.shape[0]
    head_count = queries.shape[1] // HD
    query_block = queries.reshape(query_count, head_count, HD)
    query_pos = true_position(query_ids, span_order)
    query_doc = doc_lookup(query_pos, doc_ids)
    folder = make_folder(query_block, query_pos, query_doc, span_order, doc_ids)
    initial = (
        jnp.full((head_count, query_count), NEGATIVE, jnp.float32),
        jnp.zeros((head_count, query_count), jnp.float32),
        jnp.zeros((query_count, head_count, HD), jnp.float32),
    )
    group_keys, group_values = (
        lax.all_gather(keys, "sp", axis=0, tiled=True),
        lax.all_gather(values, "sp", axis=0, tiled=True),
    )
    final = folder(
        initial,
        (
            lax.all_gather(group_keys, "cp", axis=0, tiled=True),
            lax.all_gather(group_values, "cp", axis=0, tiled=True),
        ),
        jnp.int32(0),
    )
    run_max, run_total, run_accum = final
    attended = (run_accum / jnp.transpose(run_total)[:, :, None]).astype(jnp.bfloat16)
    attended = attended.reshape(query_count, head_count * HD)
    return attended


def solution(mesh):
    in_specs = (P("cp", "sp"), P(("cp", "sp"), None), P(("cp", "sp"), None), P(), P())
    out_specs = P("cp", "sp")
    return jax.shard_map(shards, mesh=mesh, in_specs=in_specs, out_specs=out_specs, check_vma=False)
```

profile of v0, /device:TPU:94, one launch (start us, length us, event | category | flops | bytes accessed | tf_op | source)
XLA Modules:
  0.0 1104.7 jit_solution(16146311559544574172)
XLA Ops:
  6.5 26.0 %all_gather.12 = bf16[256,128]{1,0:T(8,128)(2,1)} all-gather(bf16[32,128]{1,0:T(8,128)(2,1)} %param.8), channel_id=1, replica_groups=mesh['cp'=64,'sp'=8] {'sp'}, dimensions={0}, use_global_device_ids=true | all-gather | bytes 73728 | tf_op jit(solution)/shard_map/all_gather | solution.py:89
  32.6 19.5 %all_gather.14 = bf16[256,128]{1,0:T(8,128)(2,1)} all-gather(bf16[32,128]{1,0:T(8,128)(2,1)} %param.9), channel_id=1, replica_groups=mesh['cp'=64,'sp'=8] {'sp'}, dimensions={0}, use_global_device_ids=true | all-gather | bytes 73728 | tf_op jit(solution)/shard_map/all_gather | solution.py:90
  55.0 337.2 %all-gather.3.cloned.1.call-done = bf16[16384,128]{1,0:T(8,128)(2,1)} async-done(((bf16[256,128]{1,0:T(8,128)(2,1)}), bf16[16384,128]{1,0:T(8,128)(2,1)}) %all-gather.3.cloned.1.call-update) | async-done | bytes 4194320 | tf_op jit(solution)/shard_map/all_gather | solution.py:95
  392.1 362.4 %all-gather.5.cloned.1.call-done = bf16[16384,128]{1,0:T(8,128)(2,1)} async-done(((bf16[256,128]{1,0:T(8,128)(2,1)}), bf16[16384,128]{1,0:T(8,128)(2,1)}) %all-gather.5.cloned.1.call-update) | async-done | bytes 4194320 | tf_op jit(solution)/shard_map/all_gather | solution.py:96
  754.5 342.6 %while.18 = (s32[]{:T(128)}, f32[2,256]{1,0:T(2,128)S(1)}, f32[2,256]{1,0:T(2,128)S(1)}, f32[256,2,128]{0,2,1:T(8,128)S(1)}, s32[64]{0:T(128)S(1)}, /*index=5*/s...) while((s32[]{:T(128)}, f32[2,256]{1,0:T(2,128)S(1)}, ...), condition=%wide.region_7.8_spmd.clone, body=%wide.region_2.7_spmd.clone.sunk | while | flops 68843264 | bytes 2668473 | solution.py:68
  758.5 1.1 fusion.43
  763.9 1.1 fusion.43
  769.2 1.1 fusion.43
  774.6 1.1 fusion.43
  779.9 1.1 fusion.43
  785.3 1.1 fusion.43
  790.6 1.1 fusion.43
  796.0 1.1 fusion.43
  801.4 1.1 fusion.43
  806.7 1.1 fusion.43
  812.1 1.1 fusion.43
  817.4 1.1 fusion.43
  822.8 1.1 fusion.43
  828.1 1.1 fusion.43
  833.5 1.1 fusion.43
  838.8 1.1 fusion.43
  844.2 1.1 fusion.43
  849.5 1.1 fusion.43
  854.9 1.1 fusion.43
  860.2 1.1 fusion.43
  865.6 1.1 fusion.43
  870.9 1.1 fusion.43
  876.3 1.1 fusion.43
  881.7 1.1 fusion.43
  887.0 1.1 fusion.43
  892.4 1.1 fusion.43
  897.7 1.1 fusion.43
  903.1 1.1 fusion.43
  908.4 1.1 fusion.43
  913.8 1.1 fusion.43
  919.1 1.1 fusion.43
  924.5 1.1 fusion.43
  929.8 1.1 fusion.43
  935.2 1.1 fusion.43
  940.5 1.1 fusion.43
  945.9 1.1 fusion.43
  951.2 1.1 fusion.43
  956.6 1.1 fusion.43
  961.9 1.1 fusion.43
  967.3 1.1 fusion.43
  972.6 1.1 fusion.43
  978.0 1.1 fusion.43
  983.4 1.1 fusion.43
  988.7 1.1 fusion.43
  994.1 1.1 fusion.43
  999.4 1.1 fusion.43
  1004.8 1.1 fusion.43
  1010.1 1.1 fusion.43
  1015.5 1.1 fusion.43
  1020.8 1.1 fusion.43
  1026.2 1.1 fusion.43
  1031.5 1.1 fusion.43
  1036.9 1.1 fusion.43
  1042.2 1.1 fusion.43
  1047.6 1.1 fusion.43
  1052.9 1.1 fusion.43
  1058.3 1.1 fusion.43
  1063.7 1.1 fusion.43
  1069.0 1.1 fusion.43
  (725 shorter events, 237.4 us)
Async XLA Ops:
  6.5 385.6 %all-gather.3.cloned.1.call-start = ((), (), s32[]{:S(2)}) async-start(), calls=%async_computation | async-start | bytes 4259840 | tf_op jit(solution)/shard_map/all_gather | solution.py:95
  32.6 721.9 %all-gather.5.cloned.1.call-start = ((), (), s32[]{:S(2)}) async-start(), calls=%async_computation.1 | async-start | bytes 4259840 | tf_op jit(solution)/shard_map/all_gather | solution.py:96
Sparse Core Ops, SparseCore 0:
  32.7 359.3 all-gather.2
  394.2 360.2 all-gather.4
where the time goes:
time: 1110 us; the launch traced here: 1100 us
  waiting for transfers between devices  700 us (63%)
  matrix products  143 us (13%)
  other arithmetic  124 us (11%)
  blocking collectives  45.5 us (4%)
  loops' own time  40.9 us (4%)
  local copies, waits for them, and re-layouts  37.8 us (3%)
  between operations  13.5 us (1%)
    all_gather x1, waiting for transfers between devices, shards(): lax.all_gather(group_values, 'cp', axis=0, tiled=True)  362 us
    all_gather x1, waiting for transfers between devices, shards(): lax.all_gather(group_keys, 'cp', axis=0, tiled=True)  337 us
    dot_general x64, matrix products, tile_step(): jnp.einsum('hrk,kd->rhd', weights.astype(jnp.bfloat16), value_tile, prefe...  73.6 us
    dot_general x64, matrix products, tile_step(): jnp.einsum('rhd,kd->hrk', query_block, key_tile, preferred_element_type=j...  69.8 us
    reduce_sum x65, other arithmetic, doc_lookup(): jnp.sum(jnp.where(block_index[:, None] == lookup[None, :], doc_ids[None,...  54.1 us
    reduce_sum x65, other arithmetic, true_position(): jnp.sum(jnp.where(span_index[:, None] == lookup[None, :], span_order[None...  48.6 us
    another operation x1, loops' own time, fold_piece(): lax.scan(tile_step, carried, (key_tiles, value_tiles, tile_ids))  40.9 us
    dynamic_slice x64, local copies, waits for them, and re-layouts, fold_piece(): lax.scan(tile_step, carried, (key_tiles, value_tiles, tile_ids))  35.8 us
  transfers between devices with their start and end apart: 2, of which 2 were waited for; matrix products, arithmetic and copies ran while one was open for 0% of the time, Pallas kernels for 0%

commit v1 on v0

--- a/solution.py
+++ b/solution.py
@@ -93,7 +93,9 @@
         initial,
         (
             lax.all_gather(group_keys, "cp", axis=0, tiled=True),
-            lax.all_gather(group_values, "cp", axis=0, tiled=True),
+            jnp.concatenate(
+                lax.all_to_all(jnp.stack([group_values] * lax.axis_size("cp")), "cp", 0, 0), axis=0
+            ),
         ),
         jnp.int32(0),
     )

time: 1110 us -> 784 us (0.71)
  waiting for transfers between devices: 700 us -> 361 us
  other arithmetic: 124 us -> 39.1 us
  blocking collectives: 45.5 us -> 129 us
    all_gather x1 -> x0, waiting for transfers between devices: 362 us -> none  [shards(): lax.all_gather(group_values, 'cp', axis=0, tiled=True)]
    all_gather x1, blocking collectives: 26 us -> 104 us  [shards(): lax.all_gather(keys, 'sp', axis=0, tiled=True)]
    reduce_sum x65, other arithmetic: 48.6 us -> 6.09 us  [true_position(): jnp.sum(jnp.where(span_index[:, None] == lookup[None, :], span_order[None...]
    reduce_sum x65, other arithmetic: 54.1 us -> 11.8 us  [doc_lookup(): jnp.sum(jnp.where(block_index[:, None] == lookup[None, :], doc_ids[None,...]
    all_gather x1, waiting for transfers between devices: 337 us -> 361 us  [shards(): lax.all_gather(group_keys, 'cp', axis=0, tiled=True)]
  transfers between devices with their start and end apart: 2 -> 2, of which waited for: 2 -> 1; matrix products, arithmetic and copies ran while one was open for 0% -> 0% of each run, Pallas kernels for 0% -> 0%
where the time goes in v1:
time: 784 us; the launch traced here: 777 us
  waiting for transfers between devices  361 us (46%)
  matrix products  143 us (18%)
  blocking collectives  129 us (16%)
  loops' own time  40.9 us (5%)
  local copies, waits for them, and re-layouts  39.5 us (5%)
  other arithmetic  39.1 us (5%)
  between operations  13.5 us (2%)
  starting transfers between devices  10.6 us (1%)
    all_gather x1, waiting for transfers between devices, shards(): lax.all_gather(group_keys, 'cp', axis=0, tiled=True)  361 us
    all_gather x1, blocking collectives, shards(): lax.all_gather(keys, 'sp', axis=0, tiled=True)  104 us
    dot_general x64, matrix products, tile_step(): jnp.einsum('hrk,kd->rhd', weights.astype(jnp.bfloat16), value_tile, prefe...  73.5 us
    dot_general x64, matrix products, tile_step(): jnp.einsum('rhd,kd->hrk', query_block, key_tile, preferred_element_type=j...  69.7 us
    another operation x1, loops' own time, fold_piece(): lax.scan(tile_step, carried, (key_tiles, value_tiles, tile_ids))  40.9 us
    dynamic_slice x64, local copies, waits for them, and re-layouts, fold_piece(): lax.scan(tile_step, carried, (key_tiles, value_tiles, tile_ids))  35.8 us
    all_gather x1, blocking collectives, shards(): lax.all_gather(values, 'sp', axis=0, tiled=True)  25 us
  transfers between devices with their start and end apart: 2, of which 1 were waited for; matrix products, arithmetic and copies ran while one was open for 0% of the time, Pallas kernels for 0%

profile of v1, /device:TPU:94, one launch (start us, length us, event | category | flops | bytes accessed | tf_op | source)
XLA Modules:
  0.0 777.1 jit_solution(10586866994038913129)
XLA Ops:
  6.5 25.0 %all_gather.11 = bf16[256,128]{1,0:T(8,128)(2,1)S(1)} all-gather(bf16[32,128]{1,0:T(8,128)(2,1)} %param.9), channel_id=1, replica_groups=mesh['cp'=64,'sp'=8] {'sp'}, dimensions={0}, use_global_device_ids=true | all-gather | bytes 73728 | tf_op jit(solution)/shard_map/all_gather | solution.py:90
  31.6 2.5 stack.2
  34.1 10.5 %all-to-all-start = ((bf16[64,256,128]{1,2,0:T(8,128)(2,1)}), bf16[64,256,128]{1,2,0:T(8,128)(2,1)}, u32[]{:S(2)}, u32[]{:S(2)}) async-start(bf16[64,256,128]{1,2,0:T(8,128)(2,1)} %stack.2), calls=%async_computation | async-start | bytes 8388608 | tf_op jit(solution)/shard_map/all_to_all | solution.py:97
  44.7 104.3 %all_gather.9 = bf16[256,128]{1,0:T(8,128)(2,1)} all-gather(bf16[32,128]{1,0:T(8,128)(2,1)S(1)} %copy-done.3), channel_id=1, replica_groups=mesh['cp'=64,'sp'=8] {'sp'}, dimensions={0}, use_global_device_ids=true | all-gather | bytes 73728 | tf_op jit(solution)/shard_map/all_gather | solution.py:89
  149.6 361.0 %all-gather.2.cloned.1.call-done = bf16[16384,128]{1,0:T(8,128)(2,1)} async-done(((bf16[256,128]{1,0:T(8,128)(2,1)}), bf16[16384,128]{1,0:T(8,128)(2,1)}) %all-gather.2.cloned.1.call-update) | async-done | bytes 4194320 | tf_op jit(solution)/shard_map/all_gather | solution.py:95
  510.6 258.8 %while.18 = (s32[]{:T(128)}, f32[2,256]{1,0:T(2,128)S(1)}, f32[2,256]{1,0:T(2,128)S(1)}, f32[256,2,128]{0,2,1:T(8,128)S(1)}, s32[64]{0:T(128)S(1)}, /*index=5*/s...) while((s32[]{:T(128)}, f32[2,256]{1,0:T(2,128)S(1)}, ...), condition=%wide.region_7.8_spmd.clone, body=%wide.region_2.7_spmd.clone.sunk | while | flops 68843264 | bytes 2668473 | solution.py:68
  513.3 1.1 fusion.43
  517.4 1.1 fusion.43
  521.4 1.1 fusion.43
  525.5 1.1 fusion.43
  529.5 1.1 fusion.43
  533.5 1.1 fusion.43
  537.6 1.1 fusion.43
  541.6 1.1 fusion.43
  545.7 1.1 fusion.43
  549.7 1.1 fusion.43
  553.8 1.1 fusion.43
  557.8 1.1 fusion.43
  561.9 1.1 fusion.43
  565.9 1.1 fusion.43
  569.9 1.1 fusion.43
  574.0 1.1 fusion.43
  578.0 1.1 fusion.43
  582.1 1.1 fusion.43
  586.1 1.1 fusion.43
  590.2 1.1 fusion.43
  594.2 1.1 fusion.43
  598.2 1.1 fusion.43
  602.3 1.1 fusion.43
  606.3 1.1 fusion.43
  610.4 1.1 fusion.43
  614.4 1.1 fusion.43
  618.5 1.1 fusion.43
  622.5 1.1 fusion.43
  626.6 1.1 fusion.43
  630.6 1.1 fusion.43
  634.6 1.1 fusion.43
  638.7 1.1 fusion.43
  642.7 1.1 fusion.43
  646.8 1.1 fusion.43
  650.8 1.1 fusion.43
  654.9 1.1 fusion.43
  658.9 1.1 fusion.43
  663.0 1.1 fusion.43
  667.0 1.1 fusion.43
  671.0 1.1 fusion.43
  675.1 1.1 fusion.43
  679.1 1.1 fusion.43
  683.2 1.1 fusion.43
  687.2 1.1 fusion.43
  691.3 1.1 fusion.43
  695.3 1.1 fusion.43
  699.4 1.1 fusion.43
  703.4 1.1 fusion.43
  707.4 1.1 fusion.43
  711.5 1.1 fusion.43
  715.5 1.1 fusion.43
  719.6 1.1 fusion.43
  723.6 1.1 fusion.43
  727.7 1.1 fusion.43
  739.8 1.1 fusion.43
  747.9 1.1 fusion.43
  756.0 1.1 fusion.43
  764.1 1.1 fusion.43
  (734 shorter events, 152.7 us)
Async XLA Ops:
  34.1 10.6 %copy-start.3 = (bf16[32,128]{1,0:T(8,128)(2,1)S(1)}, bf16[32,128]{1,0:T(8,128)(2,1)}, u32[]{:S(2)}) copy-start(bf16[32,128]{1,0:T(8,128)(2,1)} %param.8) | copy-start | bytes 24580
  34.1 114.9 %copy-start = (bf16[256,256]{1,0:T(8,128)(2,1)S(1)}, bf16[256,256]{1,0:T(8,128)(2,1)}, u32[]{:S(2)}) copy-start(bf16[256,256]{1,0:T(8,128)(2,1)} %param.7) | copy-start | bytes 393220
  34.1 115.2 %copy-start.1 = (s32[64]{0:T(128)S(1)}, s32[64]{0:T(128)}, u32[]{:S(2)}) copy-start(s32[64]{0:T(128)} %param.11) | copy-start | bytes 772
  34.1 115.3 %copy-start.2 = (s32[128]{0:T(128)S(1)}, s32[128]{0:T(128)}, u32[]{:S(2)}) copy-start(s32[128]{0:T(128)} %param.10) | copy-start | bytes 1540
  34.1 476.5 %all-to-all-start = ((bf16[64,256,128]{1,2,0:T(8,128)(2,1)}), bf16[64,256,128]{1,2,0:T(8,128)(2,1)}, u32[]{:S(2)}, u32[]{:S(2)}) async-start(bf16[64,256,128]{1,2,0:T(8,128)(2,1)} %stack.2), calls=%async_computation | async-start | bytes 8388608 | tf_op jit(solution)/shard_map/all_to_all | solution.py:97
  44.7 465.9 %all-gather.2.cloned.1.call-start = ((), (), s32[]{:S(2)}) async-start(), calls=%async_computation.1 | async-start | bytes 4259840 | tf_op jit(solution)/shard_map/all_gather | solution.py:95
Sparse Core Ops, SparseCore 0:
  149.1 361.4 all-gather.1
